TPU v7x, 128 devices: a whole 4x4x4 slice. The times are simulated.
128 devices in a mesh: sub: 32 (over x, y_hi, z), lib: 4 (over y_lo, core).
Axes of the slice: x: 4, y: 4 (y_hi: 2, y_lo: 2; y = y_hi * 2 + y_lo), z: 4, core: 2. Of those that a mesh axis runs over, the one named last changes fastest.
Arguments:
- snap_start: bfloat16 [4, 256, 128, 256], P(None, 'sub'), may hold values from -20 to 20
- snap_end: bfloat16 [4, 256, 128, 256], P(None, 'sub'), may hold values from -20 to 20
- exponents: int32 [512, 7], P('lib'), may hold values from 0 to 2, as said below
Outputs:
- coefficients: float32 [4, 512], P(None, 'lib')
- fitted: float32 [4, 16384], P(None, ('sub', 'lib'))
Inputs may be any that keep to these rules, and one draw needn't show every extreme that they name: Each row holds four field exponents of 0 to 2 with total degree 1 to 3, then three derivative orders of 0 to 2; rows are distinct, each of the 30 such monomials appears in one row whose derivative orders are all zero, and each of the four fields to the first power alone appears with derivative orders (0, 0, 1) and with (0, 1, 1).
All inputs are finite; a program needn't handle non-finite values.
Results may differ from a plain program's by a relative error of at most 0.0024.
Values may be sent and summed in bfloat16 or wider, within the bound.
A program may use at most 64 MiB of HBM per device.

v0:
```python
import jax
import jax.numpy as jnp
from jax import lax
from jax.sharding import PartitionSpec as P

STRIDE = 8
RADIUS = 8
POWER = 6
ITERS = 10
highest = lax.Precision.HIGHEST
ridge_term = 0.1
shrink = 0.05
epsilon = 1e-06


def shifted(value, axis, steps):
    count = lax.axis_size(axis)
    first, last = (max(0, -steps), min(count, count - steps))
    return lax.ppermute(value, axis, [(source, source + steps) for source in range(first, last)])


def tap_table(length, centers_count, offset):
    cell_pos = jnp.arange(length, dtype=jnp.float32)
    centers = STRIDE * jnp.arange(centers_count, dtype=jnp.float32) + offset
    scaled = (cell_pos[:, None] - centers[None, :]) / RADIUS
    inside = jnp.abs(scaled) <= 1.0
    bump_base = 1.0 - scaled * scaled
    zeroth = bump_base * bump_base * bump_base
    first_order = 6.0 * scaled * bump_base * bump_base
    second = -6.0 * bump_base * (1.0 - 5.0 * scaled * scaled)
    stacked = jnp.stack([zeroth, first_order, second])
    return jnp.where(inside[None], stacked, jnp.zeros_like(stacked))


def select_taps(tap_stack, orders):
    pick_rows = (orders[:, None] == jnp.arange(3, dtype=jnp.int32)[None, :]).astype(jnp.float32)
    return jnp.einsum("tj,jlc->tlc", pick_rows, tap_stack, precision=highest)


def monomial_block(fields, powers):
    result = None
    for channel in range(4):
        values = fields[channel].astype(jnp.float32)[None]
        power_here = powers[:, channel][:, None, None, None]
        factor = jnp.where(
            power_here == 0,
            jnp.ones_like(values),
            jnp.where(power_here == 1, values, values * values),
        )
        result = factor if channel == 0 else result * factor
    return result.astype(jnp.bfloat16)


def weak_block(theta_block, x_table, y_table, z_table, orders):
    z_taps = select_taps(z_table, orders[:, 2]).astype(jnp.bfloat16)
    reduced = jnp.einsum("txyz,tzc->txyc", theta_block, z_taps, preferred_element_type=jnp.float32)
    reduced = jnp.einsum(
        "txyc,tyb->txbc", reduced, select_taps(y_table, orders[:, 1]), precision=highest
    )
    return jnp.einsum(
        "txbc,txa->tabc", reduced, select_taps(x_table, orders[:, 0]), precision=highest
    )


def local(snap_start, snap_end, exponents):
    term_count = exponents.shape[0]
    cells_x = snap_start.shape[1]
    height = snap_start.shape[2]
    width_z = snap_start.shape[3]
    x_count = cells_x // STRIDE
    plane_rows = height // STRIDE * (width_z // STRIDE)
    y_table = tap_table(height, height // STRIDE, 0)
    z_table = tap_table(width_z, width_z // STRIDE, 0)
    rim_width = RADIUS - 1
    rim_pair = shifted(
        (snap_start[:, cells_x - rim_width :], snap_end[:, cells_x - rim_width :]), "sub", 1
    )
    first_field = jnp.concatenate([rim_pair[0], snap_start], axis=1)
    last_field = jnp.concatenate([rim_pair[1], snap_end], axis=1)
    x_table = tap_table(cells_x + rim_width, x_count, rim_width)

    def term_block(block_rows):
        theta_block = monomial_block(first_field, block_rows[:, :4])
        return weak_block(theta_block, x_table, y_table, z_table, block_rows[:, 4:])

    library = lax.map(term_block, exponents.reshape(term_count // 8, 8, 7))
    library = library.reshape(term_count, -1, plane_rows)
    change = (last_field.astype(jnp.float32) - first_field.astype(jnp.float32)).astype(jnp.bfloat16)
    targets = weak_block(change, x_table, y_table, z_table, jnp.zeros((4, 3), jnp.int32)).reshape(
        4, -1, plane_rows
    )
    library = library.reshape(term_count, -1)
    targets = targets.reshape(4, -1)
    row_count = library.shape[1]
    lib_count = lax.axis_size("lib")
    sub_count = lax.axis_size("sub")
    lib_index = lax.axis_index("lib")
    total_terms = term_count * lib_count
    total_rows = row_count * sub_count
    shard_piece = lax.all_gather(library.astype(jnp.bfloat16), "lib", axis=0, tiled=True).astype(
        jnp.float32
    )
    squares = jnp.zeros((total_terms,), jnp.float32)
    gram_block = lax.dot_general(
        library,
        shard_piece,
        (((1,), (1,)), ((), ())),
        precision=highest,
        preferred_element_type=jnp.float32,
    )
    gram_rows = gram_block
    squares = lax.dynamic_update_slice_in_dim(
        squares, jnp.sum(shard_piece * shard_piece, axis=1), jnp.int32(0), 0
    )
    gram_rows, squares = (gram_rows, squares)
    cross_terms = lax.dot_general(
        library,
        targets,
        (((1,), (1,)), ((), ())),
        precision=highest,
        preferred_element_type=jnp.float32,
    )
    target_squares = jnp.sum(targets * targets, axis=1)
    gram_rows, squares, cross_terms, target_squares = lax.psum(
        (gram_rows, squares, cross_terms, target_squares), "sub"
    )
    row_offset = lib_index * term_count

    def collect_coef(part_coef):
        return lax.all_gather(part_coef, "lib", axis=1, tiled=True)

    column_scale = jnp.sqrt(squares / total_rows + epsilon)
    target_scale = jnp.sqrt(target_squares / total_rows + epsilon)
    own_scale = lax.dynamic_slice_in_dim(column_scale, row_offset, term_count)
    own_ids = row_offset + jnp.arange(term_count, dtype=jnp.int32)
    identity_part = (own_ids[:, None] == jnp.arange(total_terms, dtype=jnp.int32)[None, :]).astype(
        jnp.float32
    )
    normal_rows = (
        gram_rows / (total_rows * own_scale[:, None] * column_scale[None, :])
        + ridge_term * identity_part
    )
    normal_cross = cross_terms / (total_rows * own_scale[:, None] * target_scale[None, :])
    vector = jnp.full((total_terms,), total_terms ** (-0.5), jnp.float32)
    magnitude = jnp.ones((), jnp.float32)
    for sweep_index in range(POWER):
        applied = lax.all_gather(
            jnp.dot(normal_rows, vector, precision=highest), "lib", axis=0, tiled=True
        )
        magnitude = jnp.sqrt(jnp.sum(applied * applied))
        vector = applied / magnitude
    step_size = 1.0 / magnitude

    def descend(sweep_index, coeffs):
        own_coef = lax.dynamic_slice_in_dim(coeffs, row_offset, term_count, 1)
        gradient = (
            lax.dot_general(
                coeffs,
                normal_rows,
                (((1,), (1,)), ((), ())),
                precision=highest,
                preferred_element_type=jnp.float32,
            )
            - normal_cross.T
        )
        moved_coef = own_coef - step_size * gradient
        shrunk = jnp.sign(moved_coef) * jnp.maximum(jnp.abs(moved_coef) - step_size * shrink, 0.0)
        return collect_coef(shrunk)

    coeffs = lax.fori_loop(0, ITERS, descend, jnp.zeros((4, total_terms), jnp.float32))
    lib_coef = lax.dynamic_slice_in_dim(coeffs, lib_index * term_count, term_count, 1)
    lib_scale = lax.dynamic_slice_in_dim(column_scale, lib_index * term_count, term_count)
    fit_terms = jnp.dot(
        lib_coef / lib_scale[None, :],
        library,
        precision=highest,
        preferred_element_type=jnp.float32,
    )
    fitted = lax.psum_scatter(fit_terms, "lib", scatter_dimension=1, tiled=True)
    return (lib_coef, fitted)


def solution(mesh):
    placed = (P(None, "sub", None, None), P(None, "sub", None, None), P("lib", None))
    return jax.shard_map(
        local,
        mesh=mesh,
        in_specs=placed,
        out_specs=(P(None, "lib"), P(None, ("sub", "lib"))),
        check_vma=False,
    )
```

profile of v0, /device:TPU:1, one launch (start us, length us, event | category | flops | bytes accessed | tf_op | source)
XLA Modules:
  0.0 1000.0 jit_solution(18005302535938893821)
XLA Ops:
  10.3 5.7 collective-permute-start
  22.3 31.5 %collective-permute-done = bf16[4,7,128,256]{3,2,1,0:T(8,128)(2,1)} collective-permute-done((bf16[4,7,128,256]{3,2,1,0:T(8,128)(2,1)}, bf16[4,7,128,256]{3,2,1,0:T(8,128)(2,1)}, u32[]{:S(2)}, u32[]{:S(2)}) %collective-permute-start) | collective-permute-done | bytes 1835040 | tf_op jit(solution)/shard_map/ppermute | solution.py:19
  55.7 37.4 %collective-permute-done.1 = bf16[4,7,128,256]{3,2,1,0:T(8,128)(2,1)} collective-permute-done((bf16[4,7,128,256]{3,2,1,0:T(8,128)(2,1)}, bf16[4,7,128,256]{3,2,1,0:T(8,128)(2,1)}, u32[]{:S(2)}, u32[]{:S(2)}) %collective-permute-start.1) | collective-permute-done | bytes 1835040 | tf_op jit(solution)/shard_map/ppermute | solution.py:19
  100.4 323.9 %while.22 = (s32[]{:T(128)}, f32[16,8,1,16,32]{4,3,2,1,0:T(8,128)S(1)}, s32[16,8,7]{2,1,0:T(8,128)S(1)}, f32[3,15,1]{1,0,2:T(4,128)S(1)}, f32[3,128,16]{1,0,2:T(...) while((s32[]{:T(128)}, f32[16,8,1,16,32]{4,3,2,1,0:T(8,128)S(1)}, ...), condition=%wide.region_1.2_spmd, body=%wide.region_0.1_spmd.sunk | while | flops 402870656 | bytes 60139724 | solution.py:86
  105.7 6.2 fusion.120
  112.2 7.4 convolution_bitcast_fusion.14
  126.0 6.2 fusion.120
  132.4 7.4 convolution_bitcast_fusion.14
  146.2 6.2 fusion.120
  152.6 7.4 convolution_bitcast_fusion.14
  166.4 6.2 fusion.120
  172.8 7.4 convolution_bitcast_fusion.14
  186.6 6.2 fusion.120
  193.1 7.4 convolution_bitcast_fusion.14
  206.8 6.2 fusion.120
  213.3 7.4 convolution_bitcast_fusion.14
  227.1 6.2 fusion.120
  233.5 7.4 convolution_bitcast_fusion.14
  247.3 6.2 fusion.120
  253.7 7.4 convolution_bitcast_fusion.14
  267.5 6.2 fusion.120
  273.9 7.4 convolution_bitcast_fusion.14
  287.7 6.2 fusion.120
  294.2 7.4 convolution_bitcast_fusion.14
  307.9 6.2 fusion.120
  314.4 7.4 convolution_bitcast_fusion.14
  328.1 6.2 fusion.120
  334.6 7.4 convolution_bitcast_fusion.14
  348.4 6.2 fusion.120
  354.8 7.4 convolution_bitcast_fusion.14
  368.6 6.2 fusion.120
  375.0 7.4 convolution_bitcast_fusion.14
  388.8 6.2 fusion.120
  395.3 7.4 convolution_bitcast_fusion.14
  409.0 6.2 fusion.120
  415.5 7.4 convolution_bitcast_fusion.14
  424.7 8.6 all_gather.26
  435.1 85.1 %all-reduce = (f32[512]{0:T(512)S(1)}, f32[128,4]{0,1:T(4,128)S(1)}, f32[4]{0:T(128)S(1)}) all-reduce(f32[512]{0:T(512)S(1)} %multiply_reduce_fusion, f32[128,4]{0,1:T(4,128)S(1)} %fusion.70, f32[4]{0:T(128)S(1)} %multiply_reduce_fusion.1), channel_id=1, replica_groups=mesh['sub'=32,'lib'=4] {'sub'}, use_global_device_ids=true, to_apply=%region_4.5 | all-reduce | flops 1028 | bytes 8224 | tf_op jit(solution)/shard_map/psum | solution.py:124
  520.6 333.6 %all-reduce.3.cloned.1.call-done = f32[128,512]{1,0:T(8,128)} async-done(((f32[128,512]{1,0:T(8,128)}), f32[128,512]{1,0:T(8,128)}) %all-reduce.3.cloned.1.call-update) | async-done | bytes 262160 | tf_op jit(solution)/shard_map/psum | solution.py:124
  855.6 27.1 %all-gather = f32[4,1,128]{2,1,0:T(1,128)S(1)} all-gather(f32[1,1,128]{2,1,0:T(1,128)S(1)} %convolution_bitcast_fusion.10), channel_id=1, replica_groups=mesh['sub'=32,'lib'=4] {'lib'}, dimensions={0}, use_global_device_ids=true | all-gather | bytes 2560 | tf_op jit(solution)/shard_map/all_gather | solution.py:147
  917.8 54.8 %while.23 = (s32[]{:T(128)}, f32[4,512]{1,0:T(4,128)S(1)}, s32[]{:T(128)}, f32[]{:T(128)}, f32[128,512]{1,0:T(8,128)S(1)}, /*index=5*/f32[128,4]{0,1:T(4,128)S(1)}, f32[]{:T(128)}, s32[]{:T(128)}) while((s32[]{:T(128)}, f32[4,512]{1,0:T(4,128)S(1)}, s32[]{:T(128)}, f32[]{:T(128)}, f32[128,512]{1,0:T(8,128)S(1)}, ...), condition=%wide.region_15.16_spmd, body=%wide.region_14.15_spmd.sunk | while | flops 3149826 | bytes 286817 | solution.py:170
  918.1 5.2 all_gather.34
  923.6 5.2 all_gather.34
  929.1 5.2 all_gather.34
  934.5 5.2 all_gather.34
  951.0 5.2 all_gather.34
  956.5 5.2 all_gather.34
  974.0 17.7 %reduce-scatter.4.cloned.1.call-done = f32[128,4]{1,0:T(8,128)} async-done(((f32[512,4]{1,0:T(8,128)}), f32[128,4]{1,0:T(8,128)}) %reduce-scatter.4.cloned.1.call-update) | async-done | bytes 2064
  (287 shorter events, 183.7 us)
Async XLA Ops:
  7.2 8.9 copy-start.3
  7.2 847.0 %all-reduce.3.cloned.1.call-start = ((), (), s32[]{:S(2)}) async-start(), calls=%async_computation.1 | async-start | bytes 524288 | tf_op jit(solution)/shard_map/psum | solution.py:124
  10.3 11.3 %copy-start.6 = (s32[128,7]{0,1:T(8,128)S(1)}, s32[128,7]{0,1:T(8,128)}, u32[]{:S(2)}) copy-start(s32[128,7]{0,1:T(8,128)} %param.9) | copy-start | bytes 10756
  10.3 43.5 %collective-permute-start = (bf16[4,7,128,256]{3,2,1,0:T(8,128)(2,1)}, bf16[4,7,128,256]{3,2,1,0:T(8,128)(2,1)}, u32[]{:S(2)}, u32[]{:S(2)}) collective-permute-start(bf16[4,7,128,256]{3,2,1,0:T(8,128)(2,1)} %slice.48), channel_id=1, source_target_pairs={{0,4},{4,8},{8,12},{12,16},{16,20},{20,24},{24,28},{28,32},{32,36}... | collective-permute-start | bytes 5505032 | tf_op jit(solution)/shard_map/ppermute | solution.py:19
  17.4 75.7 %collective-permute-start.1 = (bf16[4,7,128,256]{3,2,1,0:T(8,128)(2,1)}, bf16[4,7,128,256]{3,2,1,0:T(8,128)(2,1)}, u32[]{:S(2)}, u32[]{:S(2)}) collective-permute-start(bf16[4,7,128,256]{3,2,1,0:T(8,128)(2,1)} %slice.49), channel_id=1, source_target_pairs={{0,4},{4,8},{8,12},{12,16},{16,20},{20,24},{24,28},{28,32},{32,36}... | collective-permute-start | bytes 5505032 | tf_op jit(solution)/shard_map/ppermute | solution.py:19
  21.5 34.0 %copy-start.2 = (bf16[4,8,128,256]{3,2,1,0:T(8,128)(2,1)S(1)}, bf16[4,8,128,256]{3,2,1,0:T(8,128)(2,1)}, u32[]{:S(2)}) copy-start(bf16[4,8,128,256]{3,2,1,0:T(8,128)(2,1)} %param.7) | copy-start | bytes 6291460
  55.4 37.7 %copy-start.4 = (bf16[4,8,128,256]{3,2,1,0:T(8,128)(2,1)S(1)}, bf16[4,8,128,256]{3,2,1,0:T(8,128)(2,1)}, u32[]{:S(2)}) copy-start(bf16[4,8,128,256]{3,2,1,0:T(8,128)(2,1)} %param.8) | copy-start | bytes 6291460
  55.7 40.2 %copy-start = (bf16[4,15,128,256]{3,2,1,0:T(8,128)(2,1)}, bf16[4,15,128,256]{3,2,1,0:T(8,128)(2,1)S(1)}, u32[]{:S(2)}) copy-start(bf16[4,15,128,256]{3,2,1,0:T(8,128)(2,1)S(1)} %constant_dynamic-update-slice_fusion.1) | copy-start | bytes 11796484
  101.4 3.3 copy-start.1
  121.6 3.3 copy-start.1
  141.8 3.3 copy-start.1
  162.0 3.3 copy-start.1
  182.2 3.3 copy-start.1
  202.5 3.3 copy-start.1
  222.7 3.3 copy-start.1
  242.9 3.3 copy-start.1
  263.1 3.3 copy-start.1
  283.3 3.3 copy-start.1
  303.5 3.3 copy-start.1
  323.8 3.3 copy-start.1
  344.0 3.3 copy-start.1
  364.2 3.3 copy-start.1
  384.4 3.3 copy-start.1
  404.6 3.3 copy-start.1
  520.4 471.3 %reduce-scatter.4.cloned.1.call-start = ((), (), s32[]{:S(2)}) async-start(), calls=%async_computation.2 | async-start | bytes 327680
  972.7 20.5 %copy-start.5 = (f32[4,128]{1,0:T(4,128)}, f32[4,128]{1,0:T(4,128)S(1)}, u32[]{:S(2)}) copy-start(f32[4,128]{1,0:T(4,128)S(1)} %constant_dynamic-slice_fusion) | copy-start | bytes 6148
Sparse Core Ops, SparseCore 0:
  520.5 333.6 all-reduce.2
  974.1 17.5 reduce-scatter.3
where the time goes:
time: 1000 us
  waiting for transfers between devices  420 us (42%)
  matrix products  259 us (26%)
  blocking collectives  198 us (20%)
  other arithmetic  79.8 us (8%)
  between operations  18.6 us (2%)
  local copies, waits for them, and re-layouts  12.4 us (1%)
    psum x1, waiting for transfers between devices, local(): lax.psum((gram_rows, squares, cross_terms, target_squares), 'sub')  334 us
    dot_general x17, matrix products, weak_block(): jnp.einsum('txyc,tyb->txbc', reduced, select_taps(y_table, orders[:, 1]),...  122 us
    dot_general x17, matrix products, weak_block(): jnp.einsum('txyz,tzc->txyc', theta_block, z_taps, preferred_element_type=...  102 us
    psum x1, blocking collectives, local(): lax.psum((gram_rows, squares, cross_terms, target_squares), 'sub')  85.1 us
    broadcast_in_dim x32, other arithmetic, monomial_block(): jnp.where(power_here == 1, values, values * values)  69.6 us
    ppermute x2, waiting for transfers between devices, shifted(): lax.ppermute(value, axis, [(source, source + steps) for source in range(f...  68.9 us
    all_gather x6, blocking collectives, local(): lax.all_gather(jnp.dot(normal_rows, vector, precision=highest), 'lib', ax...  52.5 us
    all_gather x10, blocking collectives, collect_coef(): return lax.all_gather(part_coef, 'lib', axis=1, tiled=True)  52.1 us
  transfers between devices with their start and end apart: 4, of which 4 were waited for; matrix products, arithmetic and copies ran while one was open for 0% of the time, Pallas kernels for 0%

commit v1 on v0

--- a/solution.py
+++ b/solution.py
@@ -144,8 +144,14 @@
     vector = jnp.full((total_terms,), total_terms ** (-0.5), jnp.float32)
     magnitude = jnp.ones((), jnp.float32)
     for sweep_index in range(POWER):
-        applied = lax.all_gather(
-            jnp.dot(normal_rows, vector, precision=highest), "lib", axis=0, tiled=True
+        applied = jnp.concatenate(
+            lax.all_to_all(
+                jnp.stack([jnp.dot(normal_rows, vector, precision=highest)] * lax.axis_size("lib")),
+                "lib",
+                0,
+                0,
+            ),
+            axis=0,
         )
         magnitude = jnp.sqrt(jnp.sum(applied * applied))
         vector = applied / magnitude

time: 1000 us -> 920 us (0.920)
  waiting for transfers between devices: 420 us -> 335 us
    psum x1, waiting for transfers between devices: 334 us -> 243 us  [local(): lax.psum((gram_rows, squares, cross_terms, target_squares), 'sub')]
    all_gather x6 -> x0, blocking collectives: 52.5 us -> none  [local(): lax.all_gather(jnp.dot(normal_rows, vector, precision=highest), 'lib', ax...]
    all_to_all x0 -> x4, blocking collectives: none -> 46 us  [local(): lax.all_to_all(jnp.stack([jnp.dot(normal_rows, vector, precision=highest)...]
  transfers between devices with their start and end apart: 4 -> 6, of which waited for: 4 -> 6; matrix products, arithmetic and copies ran while one was open for 0% -> 1% of each run, Pallas kernels for 0% -> 0%
where the time goes in v1:
time: 920 us; the launch traced here: 919 us
  waiting for transfers between devices  335 us (36%)
  matrix products  259 us (28%)
  blocking collectives  194 us (21%)
  other arithmetic  79.3 us (9%)
  between operations  18.4 us (2%)
  starting transfers between devices  17.1 us (2%)
  local copies, waits for them, and re-layouts  13.7 us (1%)
    psum x1, waiting for transfers between devices, local(): lax.psum((gram_rows, squares, cross_terms, target_squares), 'sub')  243 us
    dot_general x17, matrix products, weak_block(): jnp.einsum('txyc,tyb->txbc', reduced, select_taps(y_table, orders[:, 1]),...  122 us
    dot_general x17, matrix products, weak_block(): jnp.einsum('txyz,tzc->txyc', theta_block, z_taps, preferred_element_type=...  102 us
    psum x1, blocking collectives, local(): lax.psum((gram_rows, squares, cross_terms, target_squares), 'sub')  86.6 us
    broadcast_in_dim x32, other arithmetic, monomial_block(): jnp.where(power_here == 1, values, values * values)  69.6 us
    ppermute x2, waiting for transfers between devices, shifted(): lax.ppermute(value, axis, [(source, source + steps) for source in range(f...  68.9 us
    all_gather x10, blocking collectives, collect_coef(): return lax.all_gather(part_coef, 'lib', axis=1, tiled=True)  52.6 us
    all_to_all x4, blocking collectives, local(): lax.all_to_all(jnp.stack([jnp.dot(normal_rows, vector, precision=highest)...  46 us
  transfers between devices with their start and end apart: 6, of which 6 were waited for; matrix products, arithmetic and copies ran while one was open for 1% of the time, Pallas kernels for 0%

profile of v1, /device:TPU:1, one launch (start us, length us, event | category | flops | bytes accessed | tf_op | source)
XLA Modules:
  0.0 918.9 jit_solution(11021275740745104497)
XLA Ops:
  10.3 5.7 collective-permute-start
  22.3 31.5 %collective-permute-done = bf16[4,7,128,256]{3,2,1,0:T(8,128)(2,1)} collective-permute-done((bf16[4,7,128,256]{3,2,1,0:T(8,128)(2,1)}, bf16[4,7,128,256]{3,2,1,0:T(8,128)(2,1)}, u32[]{:S(2)}, u32[]{:S(2)}) %collective-permute-start) | collective-permute-done | bytes 1835040 | tf_op jit(solution)/shard_map/ppermute | solution.py:19
  55.7 37.4 %collective-permute-done.1 = bf16[4,7,128,256]{3,2,1,0:T(8,128)(2,1)} collective-permute-done((bf16[4,7,128,256]{3,2,1,0:T(8,128)(2,1)}, bf16[4,7,128,256]{3,2,1,0:T(8,128)(2,1)}, u32[]{:S(2)}, u32[]{:S(2)}) %collective-permute-start.1) | collective-permute-done | bytes 1835040 | tf_op jit(solution)/shard_map/ppermute | solution.py:19
  100.4 324.1 %while.22 = (s32[]{:T(128)}, f32[16,8,1,16,32]{4,3,2,1,0:T(8,128)S(1)}, s32[16,8,7]{2,1,0:T(8,128)S(1)}, f32[3,15,1]{1,0,2:T(4,128)S(1)}, f32[3,128,16]{1,0,2:T(...) while((s32[]{:T(128)}, f32[16,8,1,16,32]{4,3,2,1,0:T(8,128)S(1)}, ...), condition=%wide.region_1.2_spmd, body=%wide.region_0.1_spmd.sunk | while | flops 402870656 | bytes 60139724 | solution.py:86
  105.7 6.2 fusion.120
  112.2 7.4 convolution_bitcast_fusion.14
  126.0 6.2 fusion.120
  132.4 7.4 convolution_bitcast_fusion.14
  146.2 6.2 fusion.120
  152.7 7.4 convolution_bitcast_fusion.14
  166.4 6.2 fusion.120
  172.9 7.4 convolution_bitcast_fusion.14
  186.7 6.2 fusion.120
  193.1 7.4 convolution_bitcast_fusion.14
  206.9 6.2 fusion.120
  213.3 7.4 convolution_bitcast_fusion.14
  227.1 6.2 fusion.120
  233.6 7.4 convolution_bitcast_fusion.14
  247.3 6.2 fusion.120
  253.8 7.4 convolution_bitcast_fusion.14
  267.6 6.2 fusion.120
  274.0 7.4 convolution_bitcast_fusion.14
  287.8 6.2 fusion.120
  294.3 7.4 convolution_bitcast_fusion.14
  308.0 6.2 fusion.120
  314.5 7.4 convolution_bitcast_fusion.14
  328.3 6.2 fusion.120
  334.7 7.4 convolution_bitcast_fusion.14
  348.5 6.2 fusion.120
  355.0 7.4 convolution_bitcast_fusion.14
  368.7 6.2 fusion.120
  375.2 7.4 convolution_bitcast_fusion.14
  389.0 6.2 fusion.120
  395.4 7.4 convolution_bitcast_fusion.14
  409.2 6.2 fusion.120
  415.6 7.4 convolution_bitcast_fusion.14
  424.9 8.6 all_gather.8
  435.4 86.6 %all-reduce = (f32[512]{0:T(512)S(1)}, f32[128,4]{0,1:T(4,128)S(1)}, f32[4]{0:T(128)S(1)}) all-reduce(f32[512]{0:T(512)S(1)} %multiply_reduce_fusion, f32[128,4]{0,1:T(4,128)S(1)} %fusion.70, f32[4]{0:T(128)S(1)} %multiply_reduce_fusion.1), channel_id=1, replica_groups=mesh['sub'=32,'lib'=4] {'sub'}, use_global_device_ids=true, to_apply=%region_4.5 | all-reduce | flops 1028 | bytes 8224 | tf_op jit(solution)/shard_map/psum | solution.py:124
  522.1 242.6 %all-reduce.3.cloned.1.call-done = f32[128,512]{1,0:T(8,128)} async-done(((f32[128,512]{1,0:T(8,128)}), f32[128,512]{1,0:T(8,128)}) %all-reduce.3.cloned.1.call-update) | async-done | bytes 262160 | tf_op jit(solution)/shard_map/psum | solution.py:124
  766.0 27.6 %all_to_all.36 = f32[4,1,128]{2,1,0:T(1,128)S(1)} all-to-all(f32[4,1,128]{2,1,0:T(1,128)S(1)} %stack.32), channel_id=1, replica_groups=mesh['sub'=32,'lib'=4] {'lib'}, dimensions={0} | all-to-all | bytes 4096 | tf_op jit(solution)/shard_map/all_to_all | solution.py:148
  795.2 6.1 all_to_all.37
  802.9 6.1 all_to_all.38
  810.6 6.1 all_to_all.39
  836.2 55.3 %while.23 = (s32[]{:T(128)}, f32[4,512]{1,0:T(4,128)S(1)}, s32[]{:T(128)}, f32[]{:T(128)}, f32[128,512]{1,0:T(8,128)S(1)}, /*index=5*/f32[128,4]{0,1:T(4,128)S(1)}, f32[]{:T(128)}, s32[]{:T(128)}) while((s32[]{:T(128)}, f32[4,512]{1,0:T(4,128)S(1)}, s32[]{:T(128)}, f32[]{:T(128)}, f32[128,512]{1,0:T(8,128)S(1)}, ...), condition=%wide.region_15.16_spmd, body=%wide.region_14.15_spmd.sunk | while | flops 3149826 | bytes 286817 | solution.py:176
  836.5 5.7 all_gather.10
  848.0 5.2 all_gather.10
  853.5 5.2 all_gather.10
  892.9 17.7 %reduce-scatter.4.cloned.1.call-done = f32[128,4]{1,0:T(8,128)} async-done(((f32[512,4]{1,0:T(8,128)}), f32[128,4]{1,0:T(8,128)}) %reduce-scatter.4.cloned.1.call-update) | async-done | bytes 2064
  (295 shorter events, 188.4 us)
Async XLA Ops:
  7.2 8.9 copy-start.3
  7.2 757.5 %all-reduce.3.cloned.1.call-start = ((), (), s32[]{:S(2)}) async-start(), calls=%async_computation.7 | async-start | bytes 524288 | tf_op jit(solution)/shard_map/psum | solution.py:124
  10.3 11.3 %copy-start.6 = (s32[128,7]{0,1:T(8,128)S(1)}, s32[128,7]{0,1:T(8,128)}, u32[]{:S(2)}) copy-start(s32[128,7]{0,1:T(8,128)} %param.9) | copy-start | bytes 10756
  10.3 43.5 %collective-permute-start = (bf16[4,7,128,256]{3,2,1,0:T(8,128)(2,1)}, bf16[4,7,128,256]{3,2,1,0:T(8,128)(2,1)}, u32[]{:S(2)}, u32[]{:S(2)}) collective-permute-start(bf16[4,7,128,256]{3,2,1,0:T(8,128)(2,1)} %slice.48), channel_id=1, source_target_pairs={{0,4},{4,8},{8,12},{12,16},{16,20},{20,24},{24,28},{28,32},{32,36}... | collective-permute-start | bytes 5505032 | tf_op jit(solution)/shard_map/ppermute | solution.py:19
  17.4 75.7 %collective-permute-start.1 = (bf16[4,7,128,256]{3,2,1,0:T(8,128)(2,1)}, bf16[4,7,128,256]{3,2,1,0:T(8,128)(2,1)}, u32[]{:S(2)}, u32[]{:S(2)}) collective-permute-start(bf16[4,7,128,256]{3,2,1,0:T(8,128)(2,1)} %slice.49), channel_id=1, source_target_pairs={{0,4},{4,8},{8,12},{12,16},{16,20},{20,24},{24,28},{28,32},{32,36}... | collective-permute-start | bytes 5505032 | tf_op jit(solution)/shard_map/ppermute | solution.py:19
  21.5 34.0 %copy-start.2 = (bf16[4,8,128,256]{3,2,1,0:T(8,128)(2,1)S(1)}, bf16[4,8,128,256]{3,2,1,0:T(8,128)(2,1)}, u32[]{:S(2)}) copy-start(bf16[4,8,128,256]{3,2,1,0:T(8,128)(2,1)} %param.7) | copy-start | bytes 6291460
  55.4 37.7 %copy-start.4 = (bf16[4,8,128,256]{3,2,1,0:T(8,128)(2,1)S(1)}, bf16[4,8,128,256]{3,2,1,0:T(8,128)(2,1)}, u32[]{:S(2)}) copy-start(bf16[4,8,128,256]{3,2,1,0:T(8,128)(2,1)} %param.8) | copy-start | bytes 6291460
  55.7 40.2 %copy-start = (bf16[4,15,128,256]{3,2,1,0:T(8,128)(2,1)}, bf16[4,15,128,256]{3,2,1,0:T(8,128)(2,1)S(1)}, u32[]{:S(2)}) copy-start(bf16[4,15,128,256]{3,2,1,0:T(8,128)(2,1)S(1)} %constant_dynamic-update-slice_fusion.1) | copy-start | bytes 11796484
  101.4 3.3 copy-start.1
  121.6 3.3 copy-start.1
  141.8 3.3 copy-start.1
  162.0 3.3 copy-start.1
  182.3 3.3 copy-start.1
  202.5 3.3 copy-start.1
  222.7 3.3 copy-start.1
  243.0 3.3 copy-start.1
  263.2 3.3 copy-start.1
  283.4 3.3 copy-start.1
  303.7 3.3 copy-start.1
  323.9 3.3 copy-start.1
  344.1 3.3 copy-start.1
  364.3 3.3 copy-start.1
  384.6 3.3 copy-start.1
  404.8 3.3 copy-start.1
  819.0 6.9 all-to-all-start.4
  828.1 6.9 all-to-all-start.5
  832.0 78.6 %reduce-scatter.4.cloned.1.call-start = ((), (), s32[]{:S(2)}) async-start(), calls=%async_computation.8 | async-start | bytes 327680
  891.6 20.5 %copy-start.5 = (f32[4,128]{1,0:T(4,128)}, f32[4,128]{1,0:T(4,128)S(1)}, u32[]{:S(2)}) copy-start(f32[4,128]{1,0:T(4,128)S(1)} %constant_dynamic-slice_fusion) | copy-start | bytes 6148
Sparse Core Ops, SparseCore 0:
  435.5 329.1 all-reduce.2
  893.0 17.5 reduce-scatter.3
